TPU v7x, 256 devices: a whole 4x4x8 slice. The times are simulated.
256 devices in a mesh: expert: 32 (over z, x), tensor: 8 (over y, core).
Axes of the slice: x: 4, y: 4, z: 8, core: 2. Of those that a mesh axis runs over, the one named last changes fastest.
Arguments:
- query_latent: bfloat16 [1024, 64, 576], P(('expert', 'tensor')), may hold values from -9 to 9
- kv_cache: bfloat16 [1024, 768, 576], P(('expert', 'tensor')), may hold values from -4 to 4
- cache_len: int32 [1024], P(('expert', 'tensor')), may hold values from 192 to 768, as said below
- value_up: bfloat16 [64, 512, 128], P('tensor'), may hold values from -0.25 to 0.25
- hidden_in: bfloat16 [1024, 7168], P('expert', 'tensor'), may hold values from -6 to 6
- norm_gain: bfloat16 [7168], P('tensor'), may hold values from 0.099609375 to 1.8984375
- expert_ids: int32 [1024, 8], P('expert'), may hold values from 0 to 29, all different within a row; in each aligned block of 32 rows (0 to 31, 32 to 63, ...) at most 18 rows name the same one
- route_weight: int32 [1024, 8], P('expert'), may hold values from 1 to 4095
- placement_plan: int32 [32], replicated, may hold values from 0 to 29, as said below
- updated_list: int32 [30], replicated, may hold values from 0 to 29, each once
- learner_gate: bfloat16 [30, 7168, 1024], P(None, 'expert', 'tensor'), may hold values from -0.0625 to 0.0625
- learner_up: bfloat16 [30, 7168, 1024], P(None, 'expert', 'tensor'), may hold values from -0.0625 to 0.0625
- learner_down: bfloat16 [30, 7168, 1024], P(None, 'expert', 'tensor'), may hold values from -0.1875 to 0.1875
Outputs:
- attn_values: bfloat16 [1024, 8192], P('expert', 'tensor')
- moe_out: bfloat16 [1024, 7168], P('expert', 'tensor')
- slot_gate: bfloat16 [32, 7168, 1024], P('expert', None, 'tensor')
Inputs may be any that keep to these rules, and one draw needn't show every extreme that they name: `cache_len`: some row has all 768 positions valid. `placement_plan`: every expert is held by one or two slots; 2 experts by two. `expert_ids`: each row names 8 different experts; among the 32 rows of one device no expert is named more than 18 times. `updated_list`: each expert once.
All inputs are finite; a program needn't handle non-finite values.
Results may differ from a plain program's by a relative error of at most 0.015.
Values may be sent and summed in bfloat16 or wider, within the bound.
No kernel may reach another device: no remote copies, remote signals or barrier semaphores. Data moves between devices by JAX's collectives and lax.ppermute only.
A program may use at most 128 MiB of HBM per device.

v0:
```python
import jax
import jax.numpy as jnp
from jax import lax
from jax.sharding import PartitionSpec as P

KVL = 512
SCORE_SCALE = 192.0 ** (-0.5)
ROUTE_SCALE = 2.5
NORM_EPSILON = 1e-06


def attend(query_latent, kv_cache, cache_len):
    scores = (
        jnp.einsum("rhc,rpc->rhp", query_latent, kv_cache, preferred_element_type=jnp.float32)
        * SCORE_SCALE
    )
    allowed = (jnp.arange(kv_cache.shape[1], dtype=jnp.int32)[None, :] < cache_len[:, None])[
        :, None, :
    ]
    scores = jnp.where(allowed, scores, -1e30)
    highest = jnp.max(scores, axis=2, keepdims=True)
    lifted = jnp.where(allowed, jnp.exp(scores - highest), 0.0)
    totals = jnp.sum(lifted, axis=2, keepdims=True)
    mixed = jnp.einsum(
        "rhp,rpc->rhc",
        lifted.astype(jnp.bfloat16),
        kv_cache[:, :, :KVL],
        preferred_element_type=jnp.float32,
    )
    return (mixed / totals).astype(jnp.bfloat16)


def route_targets(expert_ids, placement_plan, expert_total, capacity):
    row_count, choose_count = expert_ids.shape
    entries = row_count * choose_count
    slot_total = placement_plan.shape[0]
    flat_ids = expert_ids.reshape(entries)
    expert_range = jnp.arange(expert_total, dtype=jnp.int32)
    holders = (placement_plan[None, :] == expert_range[:, None]).astype(jnp.int32)
    holder_rank = jnp.cumsum(holders, axis=1) - 1
    picked = (flat_ids[:, None] == expert_range[None, :]).astype(jnp.int32)
    entry_hold = jnp.dot(picked, holders)
    entry_rank = jnp.dot(picked, holder_rank)
    matched = entry_hold * (entry_rank == 0).astype(jnp.int32)
    slot_index = jnp.sum(matched * jnp.arange(slot_total, dtype=jnp.int32)[None, :], axis=1)
    position = jnp.sum(matched * (jnp.cumsum(matched, axis=0) - 1), axis=1)
    return slot_index * capacity + position


def per_device(
    query_latent,
    kv_cache,
    cache_len,
    value_up,
    hidden_in,
    norm_gain,
    expert_ids,
    route_weight,
    placement_plan,
    updated_list,
    learner_gate,
    learner_up,
    learner_down,
):
    expert_total = updated_list.shape[0]
    entry_range = jnp.arange(expert_total, dtype=jnp.int32)
    learner_entry = jnp.sum(
        entry_range[None, :] * (updated_list[None, :] == placement_plan[:, None]).astype(jnp.int32),
        axis=1,
    )
    held_gate, held_up = (
        lax.all_to_all(
            jnp.take(learner_gate, learner_entry, axis=0),
            "expert",
            split_axis=0,
            concat_axis=1,
            tiled=True,
        ),
        lax.all_to_all(
            jnp.take(learner_up, learner_entry, axis=0),
            "expert",
            split_axis=0,
            concat_axis=1,
            tiled=True,
        ),
    )
    chosen_down = jnp.take(learner_down, learner_entry, axis=0)
    held_down = lax.all_to_all(chosen_down, "expert", split_axis=0, concat_axis=1, tiled=True)
    latent = attend(query_latent, kv_cache, cache_len)
    head_rows = lax.all_to_all(latent, "tensor", split_axis=1, concat_axis=0, tiled=True)
    projected = jnp.einsum("rhc,hcv->rhv", head_rows, value_up, preferred_element_type=jnp.float32)
    attn_values = projected.astype(jnp.bfloat16).reshape(
        head_rows.shape[0], projected.shape[1] * projected.shape[2]
    )
    row_count, choose_count = expert_ids.shape
    slot_total = placement_plan.shape[0]
    capacity = min(row_count, 2 * ((row_count * choose_count + expert_total - 1) // expert_total))
    targets = route_targets(expert_ids, placement_plan, expert_total, capacity)
    entry_row = jnp.arange(row_count * choose_count, dtype=jnp.int32) // choose_count
    whole_rows, whole_gain = (
        lax.all_gather(hidden_in, "tensor", axis=1, tiled=True),
        lax.all_gather(norm_gain.reshape(1, norm_gain.shape[0]), "tensor", axis=1, tiled=True),
    )
    widened = whole_rows.astype(jnp.float32)
    normed = (
        widened
        * lax.rsqrt(jnp.mean(widened * widened, axis=1, keepdims=True) + NORM_EPSILON)
        * whole_gain.astype(jnp.float32)
    ).astype(jnp.bfloat16)
    outbound = (
        jnp.zeros((slot_total * capacity, normed.shape[1]), jnp.bfloat16)
        .at[targets]
        .set(normed[entry_row])
    )
    arrived = lax.all_to_all(outbound, "expert", split_axis=0, concat_axis=0, tiled=True)
    gate_proj = jnp.dot(arrived, held_gate[0], preferred_element_type=jnp.float32)
    up_proj = jnp.dot(arrived, held_up[0], preferred_element_type=jnp.float32)
    activated = (jax.nn.silu(gate_proj) * up_proj).astype(jnp.bfloat16)
    partial_out = lax.dot_general(
        activated, held_down[0], (((1,), (1,)), ((), ())), preferred_element_type=jnp.float32
    )
    shared = lax.psum_scatter(
        partial_out.astype(jnp.bfloat16), "tensor", scatter_dimension=1, tiled=True
    )
    returned = lax.all_to_all(shared, "expert", split_axis=0, concat_axis=0, tiled=True)
    entry_out = (
        returned[targets].astype(jnp.float32).reshape(row_count, choose_count, returned.shape[1])
    )
    weights_float = route_weight.astype(jnp.float32)
    gates = ROUTE_SCALE * weights_float / jnp.sum(weights_float, axis=1, keepdims=True)
    moe_out = jnp.sum(gates[:, :, None] * entry_out, axis=1).astype(jnp.bfloat16)
    return (attn_values, moe_out, held_gate)


def solution(mesh):
    in_specs = (
        P(("expert", "tensor"), None, None),
        P(("expert", "tensor"), None, None),
        P(("expert", "tensor")),
        P("tensor", None, None),
        P("expert", "tensor"),
        P("tensor"),
        P("expert", None),
        P("expert", None),
        P(),
        P(),
        P(None, "expert", "tensor"),
        P(None, "expert", "tensor"),
        P(None, "expert", "tensor"),
    )
    out_specs = (P("expert", "tensor"), P("expert", "tensor"), P("expert", None, "tensor"))
    return jax.shard_map(
        per_device, mesh=mesh, in_specs=in_specs, out_specs=out_specs, check_vma=False
    )
```

profile of v0, /device:TPU:2, one launch (start us, length us, event | category | flops | bytes accessed | tf_op | source)
XLA Modules:
  0.0 589.7 jit_solution(17599667615994118623)
XLA Ops:
  7.2 0.0 copy-start
  7.2 1.0 select_reduce_fusion
  8.2 0.5 compare_and_fusion
  8.7 0.6 pad_clamp_fusion.1
  9.3 1.0 gather_fusion.1
  10.3 0.0 copy-start.4
  10.3 3.7 gather_fusion.2
  14.1 0.0 copy-done.4
  14.1 2.1 gather_fusion.3
  16.2 4.8 broadcast_select_fusion.2
  21.0 11.7 %all-to-all-start.2 = ((bf16[32,224,128]{2,1,0:T(8,128)(2,1)}), bf16[32,224,128]{2,1,0:T(8,128)(2,1)S(1)}, u32[]{:S(2)}, u32[]{:S(2)}) async-start(bf16[32,224,128]{2,1,0:T(8,128)(2,1)} %get-tuple-element.6), calls=%async_computation.2 | async-start | bytes 3670016 | tf_op jit(solution)/shard_map/all_to_all | solution.py:72
  32.7 0.1 copy.41
  32.8 0.1 eq.49
  32.9 0.0 copy-done.10
  32.9 0.2 reduce_window_sum.24
  33.1 43.4 %all-to-all-done.2 = bf16[32,224,128]{2,1,0:T(8,128)(2,1)S(1)} async-done(((bf16[32,224,128]{2,1,0:T(8,128)(2,1)}), bf16[32,224,128]{2,1,0:T(8,128)(2,1)S(1)}, u32[]{:S(2)}, u32[]{:S(2)}) %all-to-all-start.2) | async-done | bytes 1835040 | tf_op jit(solution)/shard_map/all_to_all | solution.py:72
  76.5 1.2 copy-done.2
  77.8 6.7 %all-to-all-start.3 = ((bf16[32,224,128]{2,1,0:T(8,128)(2,1)}), bf16[32,224,128]{2,1,0:T(8,128)(2,1)S(1)}, u32[]{:S(2)}, u32[]{:S(2)}) async-start(bf16[32,224,128]{2,1,0:T(8,128)(2,1)} %get-tuple-element.7), calls=%async_computation.3 | async-start | bytes 3670016 | tf_op jit(solution)/shard_map/all_to_all | solution.py:79
  84.5 0.3 convolution_compare_fusion
  84.7 0.2 convolution_select_fusion
  85.0 0.6 reduce-window.6
  85.6 0.2 slice_reduce_fusion
  85.8 13.4 %all-gather.1 = bf16[8,1,896]{2,1,0:T(2,128)(2,1)S(1)} all-gather(bf16[1,1,896]{2,1,0:T(2,128)(2,1)S(1)} %reshape.212), channel_id=2, replica_groups=mesh['expert'=32,'tensor'=8] {'tensor'}, dimensions={0}, use_global_device_ids=true | all-gather | bytes 16128 | tf_op jit(solution)/shard_map/all_gather | solution.py:102
  99.3 0.1 multiply_reduce_fusion
  99.4 13.6 %all_gather.6 = bf16[32,7168]{1,0:T(8,128)(2,1)S(1)} all-gather(bf16[32,896]{1,0:T(8,128)(2,1)S(1)} %copy-done.6), channel_id=1, replica_groups=mesh['expert'=32,'tensor'=8] {'tensor'}, dimensions={1}, use_global_device_ids=true | all-gather | bytes 516096 | tf_op jit(solution)/shard_map/all_gather | solution.py:101
  112.9 0.2 fusion.18
  113.2 0.2 fusion.20
  113.4 20.7 %scatter_custom_fusion = bf16[576,7168]{1,0:T(8,128)(2,1)} fusion(s32[256]{0:T(256)S(1)} %bitcast.65, bf16[]{:T(256)} %constant.57.clone.1, bf16[32,7168]{1,0:T(8,128)(2,1)S(1)} %fusion.20, s32[1024]{0:T(1024)S(1)} %pad_clamp_fusion.2), kind=kCustom, calls=%fused_computation.8 | custom fusion | bytes 8257538 | tf_op jit(solution)/shard_map/scatter | solution.py:113
  134.1 10.4 %all_to_all.56 = bf16[32,18,7168]{2,1,0:T(8,128)(2,1)} reshape(bf16[576,7168]{1,0:T(8,128)(2,1)} %scatter_custom_fusion) | data formatting | bytes 16515072 | tf_op jit(solution)/shard_map/all_to_all | solution.py:115
  144.5 0.0 all-to-all-done.3
  144.5 251.9 %all_to_all.72 = bf16[32,18,7168]{2,1,0:T(8,128)(2,1)} all-to-all(bf16[32,18,7168]{2,1,0:T(8,128)(2,1)} %all_to_all.56), channel_id=1, replica_groups=mesh['expert'=32,'tensor'=8] {'expert'}, dimensions={0} | all-to-all | bytes 16515072 | tf_op jit(solution)/shard_map/all_to_all | solution.py:115
  396.4 5.6 all-to-all-start.4
  402.1 0.3 reduce-scatter.4.cloned.1.call-start
  402.3 10.5 %all_to_all.58 = bf16[576,7168]{1,0:T(8,128)(2,1)} reshape(bf16[32,18,7168]{2,1,0:T(8,128)(2,1)} %all_to_all.72) | data formatting | bytes 16515072 | tf_op jit(solution)/shard_map/all_to_all | solution.py:115
  412.8 6.1 %fusion.40 = f32[576,128]{1,0:T(8,128)S(1)} fusion(bf16[576,7168]{1,0:T(8,128)(2,1)} %all_to_all.58, bf16[7168,128]{1,0:T(8,128)(2,1)} %bitcast.58), kind=kOutput, calls=%fused_computation.80 | convolution fusion | flops 1056964608 | bytes 10387456 | tf_op jit(solution)/shard_map/dot_general | solution.py:116
  419.0 27.4 %all-to-all-done.4 = bf16[32,224,128]{2,1,0:T(8,128)(2,1)} async-done(((bf16[32,224,128]{2,1,0:T(8,128)(2,1)}), bf16[32,224,128]{2,1,0:T(8,128)(2,1)}, u32[]{:S(2)}, u32[]{:S(2)}) %all-to-all-start.4) | async-done | bytes 1835040 | tf_op jit(solution)/shard_map/all_to_all | solution.py:88
  446.3 13.6 %convolution_convert_fusion = bf16[576,7168]{1,0:T(8,128)(2,1)} fusion(bf16[7168,128]{1,0:T(8,128)(2,1)} %bitcast.11, bf16[576,7168]{1,0:T(8,128)(2,1)} %all_to_all.58, bf16[7168,128]{1,0:T(8,128)(2,1)S(1)} %bitcast.57, f32[576,128]{1,0:T(8,128)S(1)} %fusion.40), kind=kOutput, calls=%fused_computation.7 | convolution fusion | flops 2118500352 | bytes 20480000 | tf_op jit(solution)/shard_map/dot_general | solution.py:119
  459.9 12.4 %copy.44 = bf16[576,7168]{0,1:T(8,128)(2,1)} copy(bf16[576,7168]{1,0:T(8,128)(2,1)} %convolution_convert_fusion) | data formatting | bytes 16515072
  472.3 0.0 reduce-scatter.4.cloned.1.call-update
  472.4 0.6 copy-done.11
  473.0 0.1 iota_compare_fusion.5
  473.1 0.3 copy-done.12
  473.3 3.0 fusion.39
  476.3 3.0 fusion.13
  479.3 0.9 copy.37
  480.2 3.6 all-to-all-start
  483.8 46.4 %reduce-scatter.4.cloned.1.call-done = bf16[896,576]{1,0:T(8,128)(2,1)} async-done(((bf16[7168,576]{1,0:T(8,128)(2,1)}), bf16[896,576]{1,0:T(8,128)(2,1)}) %reduce-scatter.4.cloned.1.call-update) | async-done | bytes 1032208
  530.2 1.7 copy.45
  531.9 1.3 all_to_all.62
  533.2 0.0 all-to-all-done
  533.2 10.2 %all-to-all-start.5 = ((bf16[32,18,896]{2,1,0:T(8,128)(2,1)}), bf16[32,18,896]{2,1,0:T(8,128)(2,1)S(1)}, u32[]{:S(2)}, u32[]{:S(2)}) async-start(bf16[32,18,896]{2,1,0:T(8,128)(2,1)} %all_to_all.62), calls=%async_computation.5 | async-start | bytes 2752512 | tf_op jit(solution)/shard_map/all_to_all | solution.py:125
  543.4 0.0 copy-done.7
  543.5 0.1 copy.40
  543.5 0.1 copy.54
  543.6 0.1 all_to_all.55
  543.7 0.3 fusion.17
  544.0 0.7 copy.55
  544.6 33.3 %all-to-all-done.5 = bf16[32,18,896]{2,1,0:T(8,128)(2,1)S(1)} async-done(((bf16[32,18,896]{2,1,0:T(8,128)(2,1)}), bf16[32,18,896]{2,1,0:T(8,128)(2,1)S(1)}, u32[]{:S(2)}, u32[]{:S(2)}) %all-to-all-start.5) | async-done | bytes 1032224 | tf_op jit(solution)/shard_map/all_to_all | solution.py:125
  578.0 0.3 all_to_all.64
  578.3 0.0 copy-start.3
  578.3 1.2 gather_fusion
  579.5 1.0 fusion.21
  580.5 1.2 copy.59
  581.7 0.9 copy-done.1
  (31 shorter events, 0.2 us)
Async XLA Ops:
  7.2 2.1 copy-start
  10.3 3.7 copy-start.4
  21.0 11.8 %copy-start.8 = (s32[32,8]{0,1:T(8,128)S(1)}, s32[32,8]{0,1:T(8,128)}, u32[]{:S(2)}) copy-start(s32[32,8]{0,1:T(8,128)} %param.21) | copy-start | bytes 3076
  21.0 11.9 %copy-start.10 = (s32[32]{0:T(128)S(1)}, s32[32]{0:T(128)}, u32[]{:S(2)}) copy-start(s32[32]{0:T(128)} %param.23) | copy-start | bytes 388
  21.0 55.5 %all-to-all-start.2 = ((bf16[32,224,128]{2,1,0:T(8,128)(2,1)}), bf16[32,224,128]{2,1,0:T(8,128)(2,1)S(1)}, u32[]{:S(2)}, u32[]{:S(2)}) async-start(bf16[32,224,128]{2,1,0:T(8,128)(2,1)} %get-tuple-element.6), calls=%async_computation.2 | async-start | bytes 3670016 | tf_op jit(solution)/shard_map/all_to_all | solution.py:72
  76.5 1.2 copy-start.2
  76.5 9.3 %copy-start.9 = (bf16[896]{0:T(1024)(128)(2,1)S(1)}, bf16[896]{0:T(1024)(128)(2,1)}, u32[]{:S(2)}) copy-start(bf16[896]{0:T(1024)(128)(2,1)} %param.20) | copy-start | bytes 5380
  76.5 22.9 %copy-start.6 = (bf16[32,896]{1,0:T(8,128)(2,1)S(1)}, bf16[32,896]{1,0:T(8,128)(2,1)}, u32[]{:S(2)}) copy-start(bf16[32,896]{1,0:T(8,128)(2,1)} %param.19) | copy-start | bytes 172036
  77.8 66.7 %all-to-all-start.3 = ((bf16[32,224,128]{2,1,0:T(8,128)(2,1)}), bf16[32,224,128]{2,1,0:T(8,128)(2,1)S(1)}, u32[]{:S(2)}, u32[]{:S(2)}) async-start(bf16[32,224,128]{2,1,0:T(8,128)(2,1)} %get-tuple-element.7), calls=%async_computation.3 | async-start | bytes 3670016 | tf_op jit(solution)/shard_map/all_to_all | solution.py:79
  396.4 49.9 %all-to-all-start.4 = ((bf16[32,224,128]{2,1,0:T(8,128)(2,1)}), bf16[32,224,128]{2,1,0:T(8,128)(2,1)}, u32[]{:S(2)}, u32[]{:S(2)}) async-start(bf16[32,224,128]{2,1,0:T(8,128)(2,1)} %get-tuple-element.8), calls=%async_computation.4 | async-start | bytes 3670016 | tf_op jit(solution)/shard_map/all_to_all | solution.py:88
  402.1 128.1 %reduce-scatter.4.cloned.1.call-start = ((), (), s32[]{:S(2)}) async-start(), calls=%async_computation.7 | async-start | bytes 10321920
  472.3 0.7 copy-start.11
  472.3 1.0 copy-start.12
  480.2 53.0 %all-to-all-start = ((bf16[4,64,512]{2,0,1:T(4,128)(2,1)}), bf16[4,64,512]{2,0,1:T(4,128)(2,1)S(1)}, u32[]{:S(2)}, u32[]{:S(2)}) async-start(bf16[4,64,512]{2,0,1:T(4,128)(2,1)} %copy.37), calls=%async_computation | async-start | bytes 524288 | tf_op jit(solution)/shard_map/all_to_all | solution.py:90
  533.2 10.3 %copy-start.7 = (s32[32,8]{0,1:T(8,128)S(1)}, s32[32,8]{0,1:T(8,128)}, u32[]{:S(2)}) copy-start(s32[32,8]{0,1:T(8,128)} %param.22) | copy-start | bytes 3076
  533.2 10.6 %copy-start.5 = (bf16[8,512,128]{2,1,0:T(8,128)(2,1)S(1)}, bf16[8,512,128]{2,1,0:T(8,128)(2,1)}, u32[]{:S(2)}) copy-start(bf16[8,512,128]{2,1,0:T(8,128)(2,1)} %param.18) | copy-start | bytes 3145732
  533.2 44.8 %all-to-all-start.5 = ((bf16[32,18,896]{2,1,0:T(8,128)(2,1)}), bf16[32,18,896]{2,1,0:T(8,128)(2,1)S(1)}, u32[]{:S(2)}, u32[]{:S(2)}) async-start(bf16[32,18,896]{2,1,0:T(8,128)(2,1)} %all_to_all.62), calls=%async_computation.5 | async-start | bytes 2752512 | tf_op jit(solution)/shard_map/all_to_all | solution.py:125
  578.3 2.2 copy-start.3
  580.5 2.1 copy-start.1
Sparse Core Ops, SparseCore 0:
  472.5 57.6 reduce-scatter.3
where the time goes:
time: 595 us; the launch traced here: 590 us
  blocking collectives  279 us (47%)
  waiting for transfers between devices  150 us (25%)
  local copies, waits for them, and re-layouts  71.8 us (12%)
  starting transfers between devices  38.2 us (6%)
  matrix products  26.5 us (4%)
  between operations  14.5 us (2%)
  other arithmetic  9.34 us (2%)
    all_to_all x1, blocking collectives, per_device(): lax.all_to_all(outbound, 'expert', split_axis=0, concat_axis=0, tiled=True)  252 us
    unnamed x2, waiting for transfers between devices  46.4 us
    all_to_all x1, waiting for transfers between devices, per_device(): lax.all_to_all(jnp.take(learner_gate, learner_entry, axis=0), 'expert', s...  43.4 us
    all_to_all x1, waiting for transfers between devices, per_device(): lax.all_to_all(shared, 'expert', split_axis=0, concat_axis=0, tiled=True)  33.3 us
    all_to_all x1, waiting for transfers between devices, per_device(): lax.all_to_all(chosen_down, 'expert', split_axis=0, concat_axis=1, tiled=...  27.4 us
    all_to_all x2, local copies, waits for them, and re-layouts, per_device(): lax.all_to_all(outbound, 'expert', split_axis=0, concat_axis=0, tiled=True)  20.9 us
    scatter x1, local copies, waits for them, and re-layouts, per_device(): outbound = jnp.zeros((slot_total * capacity, normed.shape[1]), jnp.bfloat...  20.7 us
    unnamed x31, local copies, waits for them, and re-layouts  18.5 us
  transfers between devices with their start and end apart: 6, of which 4 were waited for; matrix products, arithmetic and copies ran while one was open for 7% of the time, Pallas kernels for 0%

commit v1 on v0

--- a/solution.py
+++ b/solution.py
@@ -1,3 +1,4 @@
+import functools
 import jax
 import jax.numpy as jnp
 from jax import lax
@@ -7,6 +8,21 @@
 SCORE_SCALE = 192.0 ** (-0.5)
 ROUTE_SCALE = 2.5
 NORM_EPSILON = 1e-06
+
+
+def trace_cells(local, along_axis, join_dim, axis_no):
+    return jnp.concatenate(
+        lax.all_to_all(
+            jnp.stack(jnp.split(local, lax.axis_size(along_axis), join_dim), axis=0),
+            along_axis,
+            0,
+            0,
+        ),
+        axis=axis_no,
+    )
+
+
+supply_sites_over_axis = functools.partial(trace_cells, along_axis="expert", join_dim=0, axis_no=1)
 
 
 def attend(query_latent, kv_cache, cache_len):
@@ -85,7 +101,7 @@
         ),
     )
     chosen_down = jnp.take(learner_down, learner_entry, axis=0)
-    held_down = lax.all_to_all(chosen_down, "expert", split_axis=0, concat_axis=1, tiled=True)
+    held_down = supply_sites_over_axis(chosen_down)
     latent = attend(query_latent, kv_cache, cache_len)
     head_rows = lax.all_to_all(latent, "tensor", split_axis=1, concat_axis=0, tiled=True)
     projected = jnp.einsum("rhc,hcv->rhv", head_rows, value_up, preferred_element_type=jnp.float32)

time: 595 us -> 614 us (1.032)
  local copies, waits for them, and re-layouts: 71.8 us -> 91.9 us
    all_to_all x1, waiting for transfers between devices: 43.4 us -> 0.01 us  [per_device(): lax.all_to_all(jnp.take(learner_gate, learner_entry, axis=0), 'expert', s...]
    all_to_all x1, waiting for transfers between devices: 0.01 us -> 27.3 us  [per_device(): lax.all_to_all(jnp.take(learner_up, learner_entry, axis=0), 'expert', spl...]
    unnamed x31 -> x64, local copies, waits for them, and re-layouts: 18.5 us -> 37.8 us
    all_to_all x1, waiting for transfers between devices: 27.4 us -> 43.4 us  [trace_cells(): lax.all_to_all(jnp.stack(jnp.split(local, lax.axis_size(along_axis), join...]
  transfers between devices with their start and end apart: 6 -> 6, of which waited for: 4 -> 4; matrix products, arithmetic and copies ran while one was open for 7% -> 6% of each run, Pallas kernels for 0% -> 0%
where the time goes in v1:
time: 614 us; the launch traced here: 609 us
  blocking collectives  279 us (45%)
  waiting for transfers between devices  150 us (24%)
  local copies, waits for them, and re-layouts  91.9 us (15%)
  starting transfers between devices  38.1 us (6%)
  matrix products  26.5 us (4%)
  between operations  14.5 us (2%)
  other arithmetic  9.08 us (1%)
    all_to_all x1, blocking collectives, per_device(): lax.all_to_all(outbound, 'expert', split_axis=0, concat_axis=0, tiled=True)  252 us
    unnamed x2, waiting for transfers between devices  46.4 us
    all_to_all x1, waiting for transfers between devices, trace_cells(): lax.all_to_all(jnp.stack(jnp.split(local, lax.axis_size(along_axis), join...  43.4 us
    unnamed x64, local copies, waits for them, and re-layouts  37.8 us
    all_to_all x1, waiting for transfers between devices, per_device(): lax.all_to_all(shared, 'expert', split_axis=0, concat_axis=0, tiled=True)  33.3 us
    all_to_all x1, waiting for transfers between devices, per_device(): lax.all_to_all(jnp.take(learner_up, learner_entry, axis=0), 'expert', spl...  27.3 us
    all_to_all x2, local copies, waits for them, and re-layouts, per_device(): lax.all_to_all(outbound, 'expert', split_axis=0, concat_axis=0, tiled=True)  20.9 us
    scatter x1, local copies, waits for them, and re-layouts, per_device(): outbound = jnp.zeros((slot_total * capacity, normed.shape[1]), jnp.bfloat...  20.7 us
  transfers between devices with their start and end apart: 6, of which 4 were waited for; matrix products, arithmetic and copies ran while one was open for 6% of the time, Pallas kernels for 0%

profile of v1, /device:TPU:2, one launch (start us, length us, event | category | flops | bytes accessed | tf_op | source)
XLA Modules:
  0.0 609.4 jit_solution(7263334805345788320)
XLA Ops:
  7.2 1.0 select_reduce_fusion
  9.3 1.0 gather_fusion.1
  10.3 3.7 gather_fusion.2
  14.1 2.2 gather_fusion.3
  16.3 4.5 broadcast_select_fusion.2
  20.8 0.6 constant_dynamic-update-slice_fusion.31
  22.0 0.6 constant_dynamic-update-slice_fusion.29
  22.7 0.6 constant_dynamic-update-slice_fusion.28
  23.3 0.6 constant_dynamic-update-slice_fusion.27
  23.9 0.6 constant_dynamic-update-slice_fusion.26
  24.5 0.6 constant_dynamic-update-slice_fusion.25
  25.2 0.6 constant_dynamic-update-slice_fusion.24
  26.4 0.6 constant_dynamic-update-slice_fusion.22
  27.0 0.6 constant_dynamic-update-slice_fusion.21
  27.6 0.6 constant_dynamic-update-slice_fusion.20
  28.3 0.6 constant_dynamic-update-slice_fusion.19
  28.9 0.6 constant_dynamic-update-slice_fusion.18
  29.5 0.6 constant_dynamic-update-slice_fusion.17
  30.1 0.6 constant_dynamic-update-slice_fusion.16
  30.8 0.6 constant_dynamic-update-slice_fusion.15
  31.4 0.6 constant_dynamic-update-slice_fusion.14
  32.0 0.6 constant_dynamic-update-slice_fusion.13
  32.6 0.6 constant_dynamic-update-slice_fusion.12
  33.3 0.6 constant_dynamic-update-slice_fusion.11
  33.9 0.6 constant_dynamic-update-slice_fusion.10
  34.5 0.6 constant_dynamic-update-slice_fusion.9
  35.8 0.6 constant_dynamic-update-slice_fusion.7
  36.4 0.6 constant_dynamic-update-slice_fusion.6
  37.0 0.6 constant_dynamic-update-slice_fusion.5
  37.6 0.6 constant_dynamic-update-slice_fusion.4
  38.3 0.6 constant_dynamic-update-slice_fusion.3
  38.9 0.6 constant_dynamic-update-slice_fusion.2
  39.5 0.6 constant_dynamic-update-slice_fusion.1
  40.1 0.6 constant_dynamic-update-slice_fusion
  40.8 11.7 %all-to-all-start.4 = ((bf16[32,1,224,128]{3,2,1,0:T(8,128)(2,1)}), bf16[32,1,224,128]{3,2,1,0:T(8,128)(2,1)S(1)}, u32[]{:S(2)}, u32[]{:S(2)}) async-start(bf16[32,1,224,128]{3,2,1,0:T(8,128)(2,1)} %constant_dynamic-update-slice_fusion), calls=%async_computation.4 | async-start | bytes 3670016 | tf_op jit(solution)/shard_map/all_to_all | solution.py:15
  52.9 43.4 %all-to-all-done.4 = bf16[32,1,224,128]{3,2,1,0:T(8,128)(2,1)S(1)} async-done(((bf16[32,1,224,128]{3,2,1,0:T(8,128)(2,1)}), bf16[32,1,224,128]{3,2,1,0:T(8,128)(2,1)S(1)}, u32[]{:S(2)}, u32[]{:S(2)}) %all-to-all-start.4) | async-done | bytes 1835040 | tf_op jit(solution)/shard_map/all_to_all | solution.py:15
  96.3 1.3 copy-done.4
  97.6 6.7 %all-to-all-start.2 = ((bf16[32,224,128]{2,1,0:T(8,128)(2,1)}), bf16[32,224,128]{2,1,0:T(8,128)(2,1)S(1)}, u32[]{:S(2)}, u32[]{:S(2)}) async-start(bf16[32,224,128]{2,1,0:T(8,128)(2,1)} %get-tuple-element.6), calls=%async_computation.2 | async-start | bytes 3670016 | tf_op jit(solution)/shard_map/all_to_all | solution.py:88
  105.7 13.4 %all-gather.1 = bf16[8,1,896]{2,1,0:T(2,128)(2,1)S(1)} all-gather(bf16[1,1,896]{2,1,0:T(2,128)(2,1)S(1)} %reshape.208), channel_id=2, replica_groups=mesh['expert'=32,'tensor'=8] {'tensor'}, dimensions={0}, use_global_device_ids=true | all-gather | bytes 16128 | tf_op jit(solution)/shard_map/all_gather | solution.py:118
  119.2 13.6 %all_gather.6 = bf16[32,7168]{1,0:T(8,128)(2,1)S(1)} all-gather(bf16[32,896]{1,0:T(8,128)(2,1)S(1)} %copy-done.7), channel_id=1, replica_groups=mesh['expert'=32,'tensor'=8] {'tensor'}, dimensions={1}, use_global_device_ids=true | all-gather | bytes 516096 | tf_op jit(solution)/shard_map/all_gather | solution.py:117
  133.2 20.7 %scatter_custom_fusion = bf16[576,7168]{1,0:T(8,128)(2,1)} fusion(s32[256]{0:T(256)S(1)} %bitcast.194, bf16[]{:T(256)} %constant.57.clone.1, bf16[32,7168]{1,0:T(8,128)(2,1)S(1)} %fusion.20, s32[1024]{0:T(1024)S(1)} %pad_clamp_fusion.2), kind=kCustom, calls=%fused_computation.8 | custom fusion | bytes 8257538 | tf_op jit(solution)/shard_map/scatter | solution.py:129
  153.9 10.4 %all_to_all.52 = bf16[32,18,7168]{2,1,0:T(8,128)(2,1)} reshape(bf16[576,7168]{1,0:T(8,128)(2,1)} %scatter_custom_fusion) | data formatting | bytes 16515072 | tf_op jit(solution)/shard_map/all_to_all | solution.py:131
  164.3 251.9 %all_to_all.68 = bf16[32,18,7168]{2,1,0:T(8,128)(2,1)} all-to-all(bf16[32,18,7168]{2,1,0:T(8,128)(2,1)} %all_to_all.52), channel_id=1, replica_groups=mesh['expert'=32,'tensor'=8] {'expert'}, dimensions={0} | all-to-all | bytes 16515072 | tf_op jit(solution)/shard_map/all_to_all | solution.py:131
  416.3 5.6 all-to-all-start.3
  422.1 10.5 %all_to_all.54 = bf16[576,7168]{1,0:T(8,128)(2,1)} reshape(bf16[32,18,7168]{2,1,0:T(8,128)(2,1)} %all_to_all.68) | data formatting | bytes 16515072 | tf_op jit(solution)/shard_map/all_to_all | solution.py:131
  432.6 6.1 %fusion.40 = f32[576,128]{1,0:T(8,128)S(1)} fusion(bf16[576,7168]{1,0:T(8,128)(2,1)} %all_to_all.54, bf16[7168,128]{1,0:T(8,128)(2,1)} %bitcast.186), kind=kOutput, calls=%fused_computation.144 | convolution fusion | flops 1056964608 | bytes 10387456 | tf_op jit(solution)/shard_map/dot_general | solution.py:132
  438.7 27.3 %all-to-all-done.3 = bf16[32,224,128]{2,1,0:T(8,128)(2,1)S(1)} async-done(((bf16[32,224,128]{2,1,0:T(8,128)(2,1)}), bf16[32,224,128]{2,1,0:T(8,128)(2,1)S(1)}, u32[]{:S(2)}, u32[]{:S(2)}) %all-to-all-start.3) | async-done | bytes 1835040 | tf_op jit(solution)/shard_map/all_to_all | solution.py:95
  466.0 13.6 %convolution_convert_fusion = bf16[576,7168]{1,0:T(8,128)(2,1)} fusion(bf16[7168,128]{1,0:T(8,128)(2,1)} %bitcast.188, bf16[576,7168]{1,0:T(8,128)(2,1)} %all_to_all.54, bf16[7168,128]{1,0:T(8,128)(2,1)S(1)} %bitcast.185, f32[576,128]{1,0:T(8,128)S(1)} %fusion.40), kind=kOutput, calls=%fused_computation.7 | convolution fusion | flops 2118500352 | bytes 20480000 | tf_op jit(solution)/shard_map/dot_general | solution.py:135
  479.7 12.4 %copy.44 = bf16[576,7168]{0,1:T(8,128)(2,1)} copy(bf16[576,7168]{1,0:T(8,128)(2,1)} %convolution_convert_fusion) | data formatting | bytes 16515072
  492.1 0.6 copy-done.12
  493.0 3.0 fusion.39
  496.0 3.0 fusion.13
  499.0 0.9 copy.37
  499.9 3.6 all-to-all-start
  503.5 46.4 %reduce-scatter.4.cloned.1.call-done = bf16[896,576]{1,0:T(8,128)(2,1)} async-done(((bf16[7168,576]{1,0:T(8,128)(2,1)}), bf16[896,576]{1,0:T(8,128)(2,1)}) %reduce-scatter.4.cloned.1.call-update) | async-done | bytes 1032208
  549.9 1.7 copy.45
  551.6 1.3 all_to_all.58
  552.9 10.2 %all-to-all-start.5 = ((bf16[32,18,896]{2,1,0:T(8,128)(2,1)}), bf16[32,18,896]{2,1,0:T(8,128)(2,1)S(1)}, u32[]{:S(2)}, u32[]{:S(2)}) async-start(bf16[32,18,896]{2,1,0:T(8,128)(2,1)} %all_to_all.58), calls=%async_computation.5 | async-start | bytes 2752512 | tf_op jit(solution)/shard_map/all_to_all | solution.py:141
  563.7 0.7 copy.55
  564.4 33.3 %all-to-all-done.5 = bf16[32,18,896]{2,1,0:T(8,128)(2,1)S(1)} async-done(((bf16[32,18,896]{2,1,0:T(8,128)(2,1)}), bf16[32,18,896]{2,1,0:T(8,128)(2,1)S(1)}, u32[]{:S(2)}, u32[]{:S(2)}) %all-to-all-start.5) | async-done | bytes 1032224 | tf_op jit(solution)/shard_map/all_to_all | solution.py:141
  598.0 1.2 gather_fusion
  599.2 1.0 fusion.21
  600.2 1.2 copy.90
  601.4 0.9 copy-done.1
  (65 shorter events, 6.8 us)
Async XLA Ops:
  7.2 2.1 copy-start
  10.3 3.7 copy-start.5
  40.8 11.8 %copy-start.9 = (s32[32,8]{0,1:T(8,128)S(1)}, s32[32,8]{0,1:T(8,128)}, u32[]{:S(2)}) copy-start(s32[32,8]{0,1:T(8,128)} %param.21) | copy-start | bytes 3076
  40.8 11.9 %copy-start.11 = (s32[32]{0:T(128)S(1)}, s32[32]{0:T(128)}, u32[]{:S(2)}) copy-start(s32[32]{0:T(128)} %param.23) | copy-start | bytes 388
  40.8 55.5 %all-to-all-start.4 = ((bf16[32,1,224,128]{3,2,1,0:T(8,128)(2,1)}), bf16[32,1,224,128]{3,2,1,0:T(8,128)(2,1)S(1)}, u32[]{:S(2)}, u32[]{:S(2)}) async-start(bf16[32,1,224,128]{3,2,1,0:T(8,128)(2,1)} %constant_dynamic-update-slice_fusion), calls=%async_computation.4 | async-start | bytes 3670016 | tf_op jit(solution)/shard_map/all_to_all | solution.py:15
  96.3 1.3 copy-start.4
  96.3 9.3 %copy-start.10 = (bf16[896]{0:T(1024)(128)(2,1)S(1)}, bf16[896]{0:T(1024)(128)(2,1)}, u32[]{:S(2)}) copy-start(bf16[896]{0:T(1024)(128)(2,1)} %param.20) | copy-start | bytes 5380
  96.3 22.9 %copy-start.7 = (bf16[32,896]{1,0:T(8,128)(2,1)S(1)}, bf16[32,896]{1,0:T(8,128)(2,1)}, u32[]{:S(2)}) copy-start(bf16[32,896]{1,0:T(8,128)(2,1)} %param.19) | copy-start | bytes 172036
  97.6 66.7 %all-to-all-start.2 = ((bf16[32,224,128]{2,1,0:T(8,128)(2,1)}), bf16[32,224,128]{2,1,0:T(8,128)(2,1)S(1)}, u32[]{:S(2)}, u32[]{:S(2)}) async-start(bf16[32,224,128]{2,1,0:T(8,128)(2,1)} %get-tuple-element.6), calls=%async_computation.2 | async-start | bytes 3670016 | tf_op jit(solution)/shard_map/all_to_all | solution.py:88
  164.3 251.9 %copy-start.2 = (bf16[32,224,128]{2,1,0:T(8,128)(2,1)}, bf16[32,224,128]{2,1,0:T(8,128)(2,1)S(1)}, u32[]{:S(2)}) copy-start(bf16[32,224,128]{2,1,0:T(8,128)(2,1)S(1)} %all-to-all-done.2) | copy-start | bytes 5505028
  416.3 49.8 %all-to-all-start.3 = ((bf16[32,224,128]{2,1,0:T(8,128)(2,1)}), bf16[32,224,128]{2,1,0:T(8,128)(2,1)S(1)}, u32[]{:S(2)}, u32[]{:S(2)}) async-start(bf16[32,224,128]{2,1,0:T(8,128)(2,1)} %get-tuple-element.7), calls=%async_computation.3 | async-start | bytes 3670016 | tf_op jit(solution)/shard_map/all_to_all | solution.py:95
  421.8 128.1 %reduce-scatter.4.cloned.1.call-start = ((), (), s32[]{:S(2)}) async-start(), calls=%async_computation.7 | async-start | bytes 10321920
  492.1 0.7 copy-start.12
  492.1 1.0 copy-start.13
  499.9 53.0 %all-to-all-start = ((bf16[4,64,512]{2,0,1:T(4,128)(2,1)}), bf16[4,64,512]{2,0,1:T(4,128)(2,1)S(1)}, u32[]{:S(2)}, u32[]{:S(2)}) async-start(bf16[4,64,512]{2,0,1:T(4,128)(2,1)} %copy.37), calls=%async_computation | async-start | bytes 524288 | tf_op jit(solution)/shard_map/all_to_all | solution.py:106
  552.9 10.3 %copy-start.8 = (s32[32,8]{0,1:T(8,128)S(1)}, s32[32,8]{0,1:T(8,128)}, u32[]{:S(2)}) copy-start(s32[32,8]{0,1:T(8,128)} %param.22) | copy-start | bytes 3076
  552.9 10.6 %copy-start.6 = (bf16[8,512,128]{2,1,0:T(8,128)(2,1)S(1)}, bf16[8,512,128]{2,1,0:T(8,128)(2,1)}, u32[]{:S(2)}) copy-start(bf16[8,512,128]{2,1,0:T(8,128)(2,1)} %param.18) | copy-start | bytes 3145732
  552.9 44.8 %all-to-all-start.5 = ((bf16[32,18,896]{2,1,0:T(8,128)(2,1)}), bf16[32,18,896]{2,1,0:T(8,128)(2,1)S(1)}, u32[]{:S(2)}, u32[]{:S(2)}) async-start(bf16[32,18,896]{2,1,0:T(8,128)(2,1)} %all_to_all.58), calls=%async_computation.5 | async-start | bytes 2752512 | tf_op jit(solution)/shard_map/all_to_all | solution.py:141
  598.0 2.2 copy-start.3
  600.2 2.1 copy-start.1
Sparse Core Ops, SparseCore 0:
  492.2 57.6 reduce-scatter.3
